TPU v7x, 256 devices: a whole 4x4x8 slice. The times are simulated.
256 devices in a mesh: speech: 16 (over z_hi, y, core), text: 16 (over z_lo, x).
Axes of the slice: x: 4, y: 4, z: 8 (z_hi: 2, z_lo: 4; z = z_hi * 4 + z_lo), core: 2. Of those that a mesh axis runs over, the one named last changes fastest.
Arguments:
- speech_feat: float32 [8192, 512], P('speech', 'text'), may hold values from -4 to 4
- text_feat: float32 [32768, 512], P(('text', 'speech')), may hold values from -4 to 4
- text_pot: float32 [32768], P('text'), may hold values from -1 to 1
- map_grad: float32 [8192, 512], P('speech', 'text'), may hold values from -1024 to 1024
Outputs:
- speech_grad: float32 [8192, 512], P('speech', 'text')
- text_grad: float32 [32768, 512], P(('text', 'speech'))
All inputs are finite; a program needn't handle non-finite values.
Results may differ from a plain program's by a relative error of at most 0.0003.
Values sent between devices are 32-bit elements; how exact they have to be, the bound alone decides.
A program may use at most 64 MiB of HBM per device.

v0:
```python
import math

import jax
import jax.numpy as jnp
from jax import lax
from jax.experimental import pallas as pl
from jax.experimental.pallas import tpu as pltpu
from jax.sharding import PartitionSpec as P

D = 512
F = 512
T = 2048
TB = 128
SCALE = 1.0 / math.sqrt(D)
BF = jnp.bfloat16
F32 = jnp.float32
MESH = pl.DeviceIdType.MESH

NAMES = (
    ["z1", "z2", "z3"]
    + [f"{k}{r}" for r in range(4) for k in ("xp", "xm", "fp", "fm")]
    + ["za", "zb", "zaf", "zbf"]
    + [f"{k}{q}" for q in range(2) for k in ("yp", "ym", "fyp", "fym", "sb0", "sb1", "sb2", "sb3")]
    + [f"st{k}" for k in range(1, 16)]
    + [f"cs{q}{d}" for q in range(2) for d in range(4)]
    + [f"{k}{q}" for q in range(2) for k in ("ra", "rb", "rc", "rd")]
    + ["wa", "wb", "waf", "wbf"]
    + ["ua", "ub", "uc", "ud", "v1", "v2", "v3"]
)
SEM = {name: k for k, name in enumerate(NAMES)}


def halves(v):
    hi = v.astype(BF)
    return hi, (v - hi.astype(F32)).astype(BF)


def dot(a, b):
    return lax.dot_general(a, b, (((1,), (0,)), ((), ())), preferred_element_type=F32)


def kernel(
    x_ref, g_ref, t_ref, pot_ref, sg_ref, tg_ref,
    xg, tb, xh, xl, tth, ttl, rh, rl, potb, pm, gdm, wh, wl, acc, st,
    cp, sbuf, ys, ry2, ry1, rla, rlb, rla2, rlb2, zr,
    sp, xs, rx2, rx1, rz,
    ssem, rsem, lsem,
):
    s_me = lax.axis_index("speech")
    t_me = lax.axis_index("text")
    zh, y, c = s_me // 8, (s_me // 2) % 4, s_me % 2
    zl, x = t_me // 4, t_me % 4
    z = zh * 4 + zl

    def dev(zh_, y_, c_, zl_, x_):
        return {"speech": (zh_ * 4 + y_) * 2 + c_, "text": zl_ * 4 + x_}

    def at_z(zz):
        return dev(zz // 4, y, c, zz % 4, x)

    yp_, ym_ = (y + 1) % 4, (y + 3) % 4
    xp_, xm_ = (x + 1) % 4, (x + 3) % 4
    sib = dev(zh, y, 1 - c, zl, x)
    up_y, dn_y = dev(zh, yp_, c, zl, x), dev(zh, ym_, c, zl, x)
    up_x, dn_x = dev(zh, y, c, zl, xp_), dev(zh, y, c, zl, xm_)
    up_z, dn_z = at_z((z + 2) % 8), at_z((z + 6) % 8)
    pending = []

    def copy(name, src, dst, to):
        k = SEM[name]
        return pltpu.make_async_remote_copy(
            src_ref=src, dst_ref=dst, send_sem=ssem.at[k], recv_sem=rsem.at[k], device_id=to, device_id_type=MESH
        )

    def send(name, src, dst, to):
        one = copy(name, src, dst, to)
        one.start()
        pending.append(one)

    def got(name, ref):
        copy(name, ref, ref, sib).wait_recv()

    def xg_at(zl_, x_, lo=0, n=32):
        return xg.at[pl.ds(pl.multiple_of((zl_ * 4 + x_) * 32 + lo, 16), n), :]

    def tb_at(zh_, y_, c_, lo=0, n=TB):
        return tb.at[pl.ds(pl.multiple_of(((zh_ * 4 + y_) * 2 + c_) * TB + lo, 64), n), :]

    own_rows = pl.ds(pl.multiple_of(t_me * 32, 32), 32)
    local = [
        pltpu.make_async_copy(x_ref, xg.at[own_rows, pl.ds(0, F)], lsem.at[0]),
        pltpu.make_async_copy(g_ref, xg.at[own_rows, pl.ds(F, F)], lsem.at[1]),
        pltpu.make_async_copy(t_ref, tb_at(zh, y, c), lsem.at[2]),
    ]
    for one in local:
        one.start()
    barrier = pltpu.get_barrier_semaphore()
    text_peers = []
    for k in range(1, 16):
        to = {"speech": s_me, "text": (t_me + k) % 16}
        text_peers.append(to)
        pl.semaphore_signal(barrier, inc=1, device_id=to, device_id_type=MESH)
    for to in (sib, up_y, dn_y, up_z, dn_z):
        pl.semaphore_signal(barrier, inc=1, device_id=to, device_id_type=MESH)
    for one in local:
        one.wait()
    pl.semaphore_wait(barrier, 20)

    def z_send(r):
        send(f"z{r}", xg_at(zl, x), xg_at(zl, x), dev(zh, y, c, (zl + r) % 4, x))

    def x_send(r):
        zs = (zl + 4 - r) % 4
        send(f"xp{r}", xg_at(zs, x), xg_at(zs, x), up_x)
        send(f"xm{r}", xg_at(zs, x), xg_at(zs, x), dn_x)

    def x_forward(r):
        zs = (zl + 4 - r) % 4
        got(f"xp{r}", xg_at(zs, xm_))
        send(f"fp{r}", xg_at(zs, xm_, 0, 16), xg_at(zs, xm_, 0, 16), up_x)
        got(f"xm{r}", xg_at(zs, xp_))
        send(f"fm{r}", xg_at(zs, xp_, 16, 16), xg_at(zs, xp_, 16, 16), dn_x)

    def x_last(r):
        zs, x2 = (zl + 4 - r) % 4, (x + 2) % 4
        got(f"fp{r}", xg_at(zs, x2, 0, 16))
        got(f"fm{r}", xg_at(zs, x2, 16, 16))

    def zq_of(q):
        return zh if q == 0 else 1 - zh

    def y_send(q):
        zq = zq_of(q)
        send(f"yp{q}", tb_at(zq, y, c), tb_at(zq, y, c), up_y)
        send(f"ym{q}", tb_at(zq, y, c), tb_at(zq, y, c), dn_y)
        send(f"sb0{q}", tb_at(zq, y, c), tb_at(zq, y, c), sib)

    def y_forward(q):
        zq = zq_of(q)
        got(f"yp{q}", tb_at(zq, ym_, c))
        send(f"fyp{q}", tb_at(zq, ym_, c, 0, 64), tb_at(zq, ym_, c, 0, 64), up_y)
        send(f"sb1{q}", tb_at(zq, ym_, c), tb_at(zq, ym_, c), sib)
        got(f"ym{q}", tb_at(zq, yp_, c))
        send(f"fym{q}", tb_at(zq, yp_, c, 64, 64), tb_at(zq, yp_, c, 64, 64), dn_y)
        send(f"sb2{q}", tb_at(zq, yp_, c), tb_at(zq, yp_, c), sib)

    def y_last(q):
        zq, y2 = zq_of(q), (y + 2) % 4
        got(f"fyp{q}", tb_at(zq, y2, c, 0, 64))
        got(f"fym{q}", tb_at(zq, y2, c, 64, 64))
        send(f"sb3{q}", tb_at(zq, y2, c), tb_at(zq, y2, c), sib)

    def sib_got(q, k):
        zq = zq_of(q)
        got(f"sb{k}{q}", tb_at(zq, (y, ym_, yp_, (y + 2) % 4)[k], 1 - c))

    for r in (1, 2, 3):
        z_send(r)
    x_send(0)
    send("za", tb_at(zh, y, c, 0, 64), rla, up_z)
    send("zb", tb_at(zh, y, c, 64, 64), rlb, dn_z)
    y_send(0)

    def pot_step(k, _):
        row = jnp.broadcast_to(pot_ref[pl.ds(k, 1), :], (128, 128))
        potb[pl.ds(pl.multiple_of(k * 128, 128), 128), :] = jnp.transpose(row)
        return 0

    lax.fori_loop(0, 16, pot_step, 0)

    got("z1", xg_at((zl + 3) % 4, x))
    x_send(1)
    x_forward(0)
    zo_dn, zo_up = (z + 6) % 8, (z + 2) % 8
    got("za", rla)
    send("zaf", rla, tb_at(zo_dn // 4, y, c, 0, 64), up_z)
    got("zb", rlb)
    send("zbf", rlb, tb_at(zo_up // 4, y, c, 64, 64), dn_z)
    got("z2", xg_at((zl + 2) % 4, x))
    x_send(2)
    got("z3", xg_at((zl + 1) % 4, x))
    x_send(3)
    y_forward(0)
    x_forward(1)
    got("zaf", tb_at(1 - zh, y, c, 0, 64))
    got("zbf", tb_at(1 - zh, y, c, 64, 64))
    y_send(1)

    def prep_rows(r0):
        tt = jnp.transpose(tb[pl.ds(r0, 256), :])
        hi, lo = halves(tt)
        tth[:, pl.ds(r0, 256)] = hi
        ttl[:, pl.ds(r0, 256)] = lo

    def row0(zq, yy):
        return pl.multiple_of((zq * 4 + yy) * 256, 256)

    x_forward(2)
    x_forward(3)
    y_last(0)
    for k in range(4):
        sib_got(0, k)

    def prep0(k, _):
        prep_rows(row0(zh, k))
        return 0

    lax.fori_loop(0, 4, prep0, 0)
    y_forward(1)
    for r in range(4):
        x_last(r)

    def split_x(k, _):
        rows = pl.ds(pl.multiple_of(k * 64, 64), 64)
        hi, lo = halves(xg[rows, :])
        xh[rows, :] = hi
        xl[rows, :] = lo
        return 0

    lax.fori_loop(0, 8, split_x, 0)

    acc[...] = jnp.zeros_like(acc)

    def plan_rows(r0):
        rows = pl.ds(r0, 256)
        hi, lo = halves(tb[rows, :])
        prod = dot(
            jnp.concatenate([hi, lo, hi], axis=1),
            jnp.concatenate([xh[...], xh[...], xl[...]], axis=0),
        )
        pot = potb[rows, :]
        p = jnp.exp(prod[:, :F] * SCALE + jnp.concatenate([pot] * 4, axis=1))
        gd = prod[:, F:]
        pm[rows, :] = p
        gdm[rows, :] = gd
        acc[0:8, :] += jnp.sum(p.reshape(32, 8, F), axis=0)
        acc[8:16, :] += jnp.sum((p * gd).reshape(32, 8, F), axis=0)

    def plan0(k, _):
        plan_rows(row0(zh, k))
        return 0

    lax.fori_loop(0, 4, plan0, 0)
    y_last(1)
    for k in range(4):
        sib_got(1, k)

    def plan1(k, _):
        plan_rows(row0(1 - zh, k))
        return 0

    lax.fori_loop(0, 4, plan1, 0)

    mine = st.at[t_me]
    mass_part = jnp.sum(acc[0:8, :], axis=0, keepdims=True)
    dots_part = jnp.sum(acc[8:16, :], axis=0, keepdims=True)
    for k in range(4):
        mine[k : k + 1, :] = mass_part[:, k * 128 : (k + 1) * 128]
        mine[k + 4 : k + 5, :] = dots_part[:, k * 128 : (k + 1) * 128]
    for k in range(1, 16):
        send(f"st{k}", mine, mine, text_peers[k - 1])

    def prep1(k, _):
        prep_rows(row0(1 - zh, k))
        return 0

    lax.fori_loop(0, 4, prep1, 0)

    def right_x(k, _):
        cols = pl.ds(pl.multiple_of(k * 128, 128), 128)
        hi, lo = halves(jnp.transpose(xg[:, cols]) * SCALE)
        rows = pl.ds(pl.multiple_of(F + k * 128, 128), 128)
        rh[rows, :] = hi
        rl[rows, :] = lo
        return 0

    def right_g(k, _):
        cols = pl.ds(pl.multiple_of(F + k * 128, 128), 128)
        hi, lo = halves(jnp.transpose(xg[:, cols]))
        rows = pl.ds(pl.multiple_of(k * 128, 128), 128)
        rh[rows, :] = hi
        rl[rows, :] = lo
        return 0

    lax.fori_loop(0, 4, right_x, 0)
    lax.fori_loop(0, 4, right_g, 0)

    for k in range(1, 16):
        got(f"st{k}", st.at[(t_me + 16 - k) % 16])
    total = jnp.sum(st[...], axis=0)
    mass = jnp.concatenate([total[k : k + 1, :] for k in range(4)], axis=1)
    inv = 1.0 / mass
    dots = jnp.concatenate([total[k : k + 1, :] for k in range(4, 8)], axis=1) / mass

    def text_block(q, d):
        zq = zq_of(q)
        yd = (y + d) % 4
        rows = pl.ds(row0(zq, yd), 256)
        sh = pm[rows, :] * inv
        w = sh * (gdm[rows, :] - dots)
        sh_hi, sh_lo = halves(sh)
        w_hi, w_lo = halves(w)
        wh[rows, :] = w_hi
        wl[rows, :] = w_lo
        out = dot(
            jnp.concatenate([sh_hi, w_hi, sh_lo, w_lo, sh_hi, w_hi], axis=1),
            jnp.concatenate([rh[...], rh[...], rl[...]], axis=0),
        )
        cp[zq, yd] = out.reshape(2, TB, D)

    def cross(q, d):
        zq, yd = zq_of(q), (y + d) % 4
        send(f"cs{q}{d}", cp.at[zq, yd, 1 - c], sbuf.at[q, d], sib)

    def text_pair(q, first):
        def step(k, _):
            text_block(q, 2 - k if first else 3 - 3 * k)
            return 0

        lax.fori_loop(0, 2, step, 0)
        for d in (2, 1) if first else (3, 0):
            cross(q, d)

    def chip_sum(q, d):
        got(f"cs{q}{d}", sbuf.at[q, d])
        return cp[zq_of(q), (y + d) % 4, c] + sbuf[q, d]

    def far_y(q):
        ys[q, 2] = chip_sum(q, 2)
        send(f"ra{q}", ys.at[q, 2, pl.ds(0, 64)], ry2.at[q, 0], up_y)
        send(f"rb{q}", ys.at[q, 2, pl.ds(64, 64)], ry2.at[q, 1], dn_y)

    def near_y(q):
        one = chip_sum(q, 1)
        got(f"ra{q}", ry2.at[q, 0])
        ys[q, 1, 0:64] = one[0:64] + ry2[q, 0]
        ys[q, 1, 64:128] = one[64:128]
        send(f"rc{q}", ys.at[q, 1], ry1.at[q, 0], up_y)
        two = chip_sum(q, 3)
        got(f"rb{q}", ry2.at[q, 1])
        ys[q, 3, 0:64] = two[0:64]
        ys[q, 3, 64:128] = two[64:128] + ry2[q, 1]
        send(f"rd{q}", ys.at[q, 3], ry1.at[q, 1], dn_y)

    def own_y(q):
        one = chip_sum(q, 0)
        got(f"rc{q}", ry1.at[q, 0])
        got(f"rd{q}", ry1.at[q, 1])
        ys[q, 0] = one + (ry1[q, 0] + ry1[q, 1])

    text_pair(1, True)
    far_y(1)
    text_pair(1, False)
    near_y(1)
    text_pair(0, True)
    far_y(0)
    text_pair(0, False)

    def speech_rows(m, _):
        rows = pl.ds(pl.multiple_of(m * 256, 256), 256)
        hi, lo = tth[rows, :], ttl[rows, :]
        out = dot(
            jnp.concatenate([hi, lo, hi], axis=1),
            jnp.concatenate([wh[...], wh[...], wl[...]], axis=0),
        )
        sp[pl.ds(m * 2, 2)] = out.reshape(2, 4, 32, F)
        return 0

    near_y(0)
    own_y(1)
    send("wa", ys.at[1, 0, pl.ds(0, 64)], rla2, up_z)
    send("wb", ys.at[1, 0, pl.ds(64, 64)], rlb2, dn_z)
    lax.fori_loop(0, 2, speech_rows, 0)
    x2 = (x + 2) % 4
    send("ua", sp.at[:, x2, pl.ds(0, 16)], rx2.at[0], up_x)
    send("ub", sp.at[:, x2, pl.ds(16, 16)], rx2.at[1], dn_x)
    got("wa", rla2)
    send("waf", rla2, zr.at[pl.ds(0, 64)], up_z)
    got("wb", rlb2)
    send("wbf", rlb2, zr.at[pl.ds(64, 64)], dn_z)
    got("ua", rx2.at[0])
    xs[0, :, 0:16] = sp[:, xp_, 0:16] + rx2[0]
    xs[0, :, 16:32] = sp[:, xp_, 16:32]
    send("uc", xs.at[0], rx1.at[0], up_x)
    got("ub", rx2.at[1])
    xs[1, :, 0:16] = sp[:, xm_, 0:16]
    xs[1, :, 16:32] = sp[:, xm_, 16:32] + rx2[1]
    send("ud", xs.at[1], rx1.at[1], dn_x)
    got("uc", rx1.at[0])
    got("ud", rx1.at[1])
    xs[2] = sp[:, x] + (rx1[0] + rx1[1])
    for r in (1, 2, 3):
        zt = (zl + r) % 4
        send(f"v{r}", xs.at[2, zt], rz.at[r - 1], dev(zh, y, c, zt, x))
    own_y(0)
    for r in (1, 2, 3):
        got(f"v{r}", rz.at[r - 1])
    sg_ref[...] = (xs[2, zl] + (rz[0] + (rz[1] + rz[2]))) * SCALE
    got("waf", zr.at[pl.ds(0, 64)])
    got("wbf", zr.at[pl.ds(64, 64)])
    tg_ref[...] = ys[0, 0] + zr[...]
    for one in pending:
        one.wait_send()


def solution(mesh):
    def v(shape, kind=F32):
        return pltpu.VMEM(shape, kind)

    scratch = [
        v((D, 2 * F)), v((T, D)), v((D, 2 * F), BF), v((D, 2 * F), BF),
        v((D, T), BF), v((D, T), BF), v((2 * F, D), BF), v((2 * F, D), BF),
        v((T, 128)), v((T, F)), v((T, F)), v((T, F), BF), v((T, F), BF), v((16, F)), v((16, 8, 128)),
        v((2, 4, 2, TB, D)), v((2, 4, TB, D)), v((2, 4, TB, D)), v((2, 2, 64, D)), v((2, 2, TB, D)),
        v((64, D)), v((64, D)), v((64, D)), v((64, D)), v((TB, D)),
        v((4, 4, 32, F)), v((3, 4, 32, F)), v((2, 4, 16, F)), v((2, 4, 32, F)), v((3, 32, F)),
        pltpu.SemaphoreType.DMA((len(NAMES),)),
        pltpu.SemaphoreType.DMA((len(NAMES),)),
        pltpu.SemaphoreType.DMA((3,)),
    ]
    anywhere = pl.BlockSpec(memory_space=pl.ANY)
    vmem = pl.BlockSpec(memory_space=pltpu.VMEM)
    call = pl.pallas_call(
        kernel,
        out_shape=(jax.ShapeDtypeStruct((32, F), F32), jax.ShapeDtypeStruct((TB, D), F32)),
        in_specs=[anywhere, anywhere, anywhere, vmem],
        out_specs=(vmem, vmem),
        scratch_shapes=scratch,
        compiler_params=pltpu.CompilerParams(
            collective_id=0, has_side_effects=True, vmem_limit_bytes=62 * 1024 * 1024
        ),
    )

    def shards(speech_feat, text_feat, text_pot, map_grad):
        sg, tg = call(speech_feat.T, map_grad.T, text_feat, text_pot.reshape(16, 128))
        return sg.T, tg

    return jax.shard_map(
        shards,
        mesh=mesh,
        in_specs=(P("speech", "text"), P(("text", "speech"), None), P("text"), P("speech", "text")),
        out_specs=(P("speech", "text"), P(("text", "speech"), None)),
        check_vma=False,
    )
```

profile of v0, /device:TPU:2, one launch (start us, length us, event | category | flops | bytes accessed | tf_op | source)
XLA Modules:
  0.0 103.3 jit_solution(7776027282408065494)
XLA Ops:
  0.6 99.5 %shard_map.59 = (f32[32,512]{1,0:T(8,128)}, f32[128,512]{1,0:T(8,128)}) custom-call(f32[32,512]{1,0:T(8,128)} %bitcast.4, f32[32,512]{1,0:T(8,128)} %bitcast.5, f32[128,512]{1,0:T(8,128)} %t_ref.1, f32[16,128]{1,0:T(8,128)} %bitcast.7), custom_call_target="tpu_custom_call" | custom-call | tf_op jit(solution)/shard_map/pallas_call | solution.py:435
  100.1 1.5 %copy.8 = f32[512,32]{0,1:T(8,128)} copy(f32[512,32]{0,1:T(8,128)} %bitcast.6) | data formatting | bytes 131072
  101.6 1.7 %copy.9 = f32[128,512]{1,0:T(8,128)} copy(f32[128,512]{1,0:T(8,128)} %get-tuple-element.9) | data formatting | bytes 524288
where the time goes:
time: 103 us
  Pallas kernels  99.5 us (97%)
  local copies, waits for them, and re-layouts  3.14 us (3%)
    pallas_call x1, Pallas kernels, shards(): call(speech_feat.T, map_grad.T, text_feat, text_pot.reshape(16, 128))  99.5 us
    unnamed x2, local copies, waits for them, and re-layouts  3.14 us

commit v1 on v0

v1 whole, which is shorter than its diff:
```python
import math

import jax
import jax.numpy as jnp
from jax import lax
from jax.experimental import pallas as pl
from jax.experimental.pallas import tpu as pltpu
from jax.sharding import PartitionSpec as P

D = 512
F = 512
T = 2048
TB = 128
SCALE = 1.0 / math.sqrt(D)
BF = jnp.bfloat16
F32 = jnp.float32
MESH = pl.DeviceIdType.MESH

NAMES = (
    [f"{k}{j}" for j in (1, 2, 3) for k in ("zu", "zd")]
    + [f"{k}{r}" for r in range(4) for k in ("xp", "xm", "fp", "fm")]
    + [f"{k}{h}{p}" for h in (1, 2, 3, 4) for p in range(2) for k in ("tu", "td")]
    + [f"{k}{q}" for q in range(3) for k in ("yp", "ym", "fyp", "fym", "sb0", "sb1", "sb2", "sb3")]
    + [f"st{k}" for k in range(1, 16)]
    + [f"cs{q}{d}" for q in range(2) for d in range(4)]
    + [f"{k}{q}{p}" for q in range(2) for p in range(2) for k in ("ra", "rb", "rc", "rd", "re", "rf")]
    + [f"w{p}" for p in range(2)]
    + [f"{k}{m}" for m in range(2) for k in ("ua", "ub", "uc", "ud", "ue", "uf")]
    + ["v1", "v2", "v3"]
)
SEM = {name: k for k, name in enumerate(NAMES)}


def halves(v):
    hi = v.astype(BF)
    return hi, (v - hi.astype(F32)).astype(BF)


def dot(a, b):
    return lax.dot_general(a, b, (((1,), (0,)), ((), ())), preferred_element_type=F32)


def kernel(
    x_ref, g_ref, t_ref, pot_ref, sg_ref, tg_ref,
    xg, tb, xh, xl, tth, ttl, rh, rl, potb, pm, gdm, wh, wl, acc, st,
    cp, sbuf, ys, ry2, ry1, zr, ru, rd,
    sp, xs, xo, rx2, rx1, rz,
    ssem, rsem, lsem,
):
    s_me = lax.axis_index("speech")
    t_me = lax.axis_index("text")
    zh, y, c = s_me // 8, (s_me // 2) % 4, s_me % 2
    zl, x = t_me // 4, t_me % 4
    z = zh * 4 + zl

    def dev(zh_, y_, c_, zl_, x_):
        return {"speech": (zh_ * 4 + y_) * 2 + c_, "text": zl_ * 4 + x_}

    def at_z(zz):
        return dev(zz // 4, y, c, zz % 4, x)

    yp_, ym_ = (y + 1) % 4, (y + 3) % 4
    xp_, xm_ = (x + 1) % 4, (x + 3) % 4
    sib = dev(zh, y, 1 - c, zl, x)
    up_y, dn_y = dev(zh, yp_, c, zl, x), dev(zh, ym_, c, zl, x)
    up_x, dn_x = dev(zh, y, c, zl, xp_), dev(zh, y, c, zl, xm_)
    far_z = at_z((z + 4) % 8)
    up_z, dn_z = at_z((z + 1) % 8), at_z((z + 7) % 8)
    pending = []

    def copy(name, src, dst, to):
        k = SEM[name]
        return pltpu.make_async_remote_copy(
            src_ref=src, dst_ref=dst, send_sem=ssem.at[k], recv_sem=rsem.at[k], device_id=to, device_id_type=MESH
        )

    def send(name, src, dst, to, track=True):
        one = copy(name, src, dst, to)
        one.start()
        if track:
            pending.append(one)

    def got(name, ref):
        copy(name, ref, ref, sib).wait_recv()

    def xg_at(zl_, x_, lo=0, n=32):
        return xg.at[pl.ds(pl.multiple_of((zl_ * 4 + x_) * 32 + lo, 16), n), :]

    def tb_at(zh_, y_, c_, lo=0, n=TB):
        return tb.at[zh_, y_, c_, pl.ds(lo, n), :]

    own_rows = pl.ds(pl.multiple_of(t_me * 32, 32), 32)
    local = [
        pltpu.make_async_copy(x_ref, xg.at[own_rows, pl.ds(0, F)], lsem.at[0]),
        pltpu.make_async_copy(g_ref, xg.at[own_rows, pl.ds(F, F)], lsem.at[1]),
        pltpu.make_async_copy(t_ref, tb_at(zh, y, c), lsem.at[2]),
    ]
    for one in local:
        one.start()
    barrier = pltpu.get_barrier_semaphore()
    text_peers = []
    for k in range(1, 16):
        to = {"speech": s_me, "text": (t_me + k) % 16}
        text_peers.append(to)
        pl.semaphore_signal(barrier, inc=1, device_id=to, device_id_type=MESH)
    for to in (sib, up_y, dn_y, far_z, up_z, dn_z):
        pl.semaphore_signal(barrier, inc=1, device_id=to, device_id_type=MESH)
    for one in local:
        one.wait()
    pl.semaphore_wait(barrier, 21)

    def line_up(j):
        block = xg_at(zl + 1 - j, x)
        return (zl <= 2) & (zl >= j - 1), copy(f"zu{j}", block, block, dev(zh, y, c, zl + 1, x))

    def line_down(j):
        block = xg_at(zl + j - 1, x)
        return (zl >= 1) & (zl <= 4 - j), copy(f"zd{j}", block, block, dev(zh, y, c, zl - 1, x))

    def line_send(j):
        for fits, one in (line_up(j), line_down(j)):

            @pl.when(fits)
            def _(one=one):
                one.start()

    def line_got(j):
        @pl.when(zl >= j)
        def _():
            got(f"zu{j}", xg_at(zl - j, x))

        @pl.when(zl <= 3 - j)
        def _():
            got(f"zd{j}", xg_at(zl + j, x))

    def line_step(j):
        line_got(j)
        if j < 3:
            line_send(j + 1)
        by_step(j, x_send)

    def by_step(j, do):
        if j == 2:
            do(2)
            return
        for r, here in ((1, zl >= 1), (3, zl <= 2)) if j == 1 else ((3, zl == 3), (1, zl == 0)):

            @pl.when(here)
            def _(r=r):
                do(r, False)

    def x_send(r, track=True):
        zs = (zl + 4 - r) % 4
        send(f"xp{r}", xg_at(zs, x), xg_at(zs, x), up_x, track)
        send(f"xm{r}", xg_at(zs, x), xg_at(zs, x), dn_x, track)

    def x_forward(r, track=True):
        zs = (zl + 4 - r) % 4
        got(f"xp{r}", xg_at(zs, xm_))
        send(f"fp{r}", xg_at(zs, xm_, 0, 16), xg_at(zs, xm_, 0, 16), up_x, track)
        got(f"xm{r}", xg_at(zs, xp_))
        send(f"fm{r}", xg_at(zs, xp_, 16, 16), xg_at(zs, xp_, 16, 16), dn_x, track)

    def x_sent(r):
        zs = (zl + 4 - r) % 4
        for name, lo, n in (("xp", 0, 32), ("xm", 0, 32), ("fp", 0, 16), ("fm", 16, 16)):
            pending.append(copy(f"{name}{r}", xg_at(zs, x, lo, n), xg_at(zs, x, lo, n), up_x))

    def x_last(r):
        zs, x2 = (zl + 4 - r) % 4, (x + 2) % 4
        got(f"fp{r}", xg_at(zs, x2, 0, 16))
        got(f"fm{r}", xg_at(zs, x2, 16, 16))

    def zq_of(q):
        return zh if q == 0 else 1 - zh

    def parcel(g):
        return (zh, 0, TB) if g == 0 else (1 - zh, (g - 1) * 64, 64)

    def y_send(g):
        zq, lo, n = parcel(g)
        send(f"yp{g}", tb_at(zq, y, c, lo, n), tb_at(zq, y, c, lo, n), up_y)
        send(f"ym{g}", tb_at(zq, y, c, lo, n), tb_at(zq, y, c, lo, n), dn_y)
        send(f"sb0{g}", tb_at(zq, y, c, lo, n), tb_at(zq, y, c, lo, n), sib)

    def y_forward(g):
        zq, lo, n = parcel(g)
        h = n // 2
        got(f"yp{g}", tb_at(zq, ym_, c, lo, n))
        send(f"fyp{g}", tb_at(zq, ym_, c, lo, h), tb_at(zq, ym_, c, lo, h), up_y)
        got(f"ym{g}", tb_at(zq, yp_, c, lo, n))
        send(f"fym{g}", tb_at(zq, yp_, c, lo + h, h), tb_at(zq, yp_, c, lo + h, h), dn_y)
        send(f"sb1{g}", tb_at(zq, ym_, c, lo, n), tb_at(zq, ym_, c, lo, n), sib)
        send(f"sb2{g}", tb_at(zq, yp_, c, lo, n), tb_at(zq, yp_, c, lo, n), sib)

    def y_last(g):
        zq, lo, n = parcel(g)
        h, y2 = n // 2, (y + 2) % 4
        got(f"fyp{g}", tb_at(zq, y2, c, lo, h))
        got(f"fym{g}", tb_at(zq, y2, c, lo + h, h))
        send(f"sb3{g}", tb_at(zq, y2, c, lo, n), tb_at(zq, y2, c, lo, n), sib)

    def sib_got(g, ks=(0, 1, 2, 3)):
        zq, lo, n = parcel(g)
        for k in ks:
            got(f"sb{k}{g}", tb_at(zq, (y, ym_, yp_, (y + 2) % 4)[k], 1 - c, lo, n))

    def t_hop(h):
        for p in range(2):
            u, d = pl.ds(64 * p, 32), pl.ds(64 * p + 32, 32)
            if h == 1:
                src_u, src_d = tb.at[zh, y, c, u], tb.at[zh, y, c, d]
            else:
                src_u, src_d = ru.at[h - 2, p], rd.at[h - 2, p]
                got(f"tu{h - 1}{p}", src_u)
                got(f"td{h - 1}{p}", src_d)
            if h == 4:
                dst_u, dst_d = tb.at[((z + 5) % 8) // 4, y, c, u], tb.at[((z + 3) % 8) // 4, y, c, d]
            else:
                dst_u, dst_d = ru.at[h - 1, p], rd.at[h - 1, p]
            send(f"tu{h}{p}", src_u, dst_u, up_z)
            send(f"td{h}{p}", src_d, dst_d, dn_z)

    def z_arrived(p):
        got(f"tu4{p}", tb_at(1 - zh, y, c, 64 * p, 32))
        got(f"td4{p}", tb_at(1 - zh, y, c, 64 * p + 32, 32))
        y_send(p + 1)

    line_send(1)
    x_send(0)
    t_hop(1)
    y_send(0)

    def pot_step(k, _):
        row = jnp.broadcast_to(pot_ref[pl.ds(k, 1), :], (128, 128))
        potb[k] = jnp.transpose(row)
        return 0

    lax.fori_loop(0, 16, pot_step, 0)

    def prep_rows(zq, yy):
        hi, lo = halves(jnp.transpose(tb[zq, yy].reshape(256, D)))
        cols = pl.ds(pl.multiple_of((zq * 4 + yy) * 256, 256), 256)
        tth[:, cols] = hi
        ttl[:, cols] = lo

    def split_x(k, _):
        rows = pl.ds(pl.multiple_of(k * 64, 64), 64)
        hi, lo = halves(xg[rows, :])
        xh[rows, :] = hi
        xl[rows, :] = lo
        return 0

    def plan_part(rows_t, pot, put):
        hi, lo = halves(rows_t)
        prod = dot(
            jnp.concatenate([hi, lo, hi], axis=1),
            jnp.concatenate([xh[...], xh[...], xl[...]], axis=0),
        )
        p = jnp.exp(prod[:, :F] * SCALE + jnp.concatenate([pot] * 4, axis=1))
        gd = prod[:, F:]
        put(p, gd)
        acc[0:8, :] += jnp.sum(p.reshape(32, 8, F), axis=0)
        acc[8:16, :] += jnp.sum((p * gd).reshape(32, 8, F), axis=0)

    def plan_block(zq, yy):
        def put(p, gd):
            pm[zq, yy] = p.reshape(2, TB, F)
            gdm[zq, yy] = gd.reshape(2, TB, F)

        pot = potb[pl.ds((zq * 4 + yy) * 2, 2)].reshape(256, 128)
        plan_part(tb[zq, yy].reshape(256, D), pot, put)

    def plan_piece(zq, two_y, p):
        rows = pl.ds(64 * p, 64)

        def put(p_, gd):
            for k, yy in enumerate(two_y):
                part = slice(128 * k, 128 * k + 128)
                pm[zq, yy, :, rows, :] = p_[part].reshape(2, 64, F)
                gdm[zq, yy, :, rows, :] = gd[part].reshape(2, 64, F)

        pot = jnp.concatenate([potb[pl.ds((zq * 4 + yy) * 2, 2), rows, :].reshape(128, 128) for yy in two_y], axis=0)
        tok = jnp.concatenate([tb[zq, yy, :, rows, :].reshape(128, D) for yy in two_y], axis=0)
        plan_part(tok, pot, put)

    def loop(n, step):
        lax.fori_loop(0, n, lambda k, _: (step(k), 0)[1], 0)

    acc[...] = jnp.zeros_like(acc)
    line_step(1)
    x_forward(0)
    t_hop(2)
    y_forward(0)
    line_step(2)
    by_step(1, x_forward)
    t_hop(3)
    y_last(0)
    line_step(3)
    by_step(2, x_forward)
    sib_got(0)
    t_hop(4)
    by_step(3, x_forward)
    loop(4, lambda k: prep_rows(zh, k))
    z_arrived(0)
    z_arrived(1)
    for r in range(4):
        x_last(r)
    for r in (1, 3):
        x_sent(r)
    lax.fori_loop(0, 8, split_x, 0)
    plan_block(zh, 0)
    y_forward(1)
    plan_block(zh, 1)
    y_forward(2)
    loop(2, lambda k: plan_block(zh, k + 2))
    sib_got(1, (0, 1))
    plan_piece(1 - zh, (y, ym_), 0)
    y_last(1)
    sib_got(2, (0, 1))
    plan_piece(1 - zh, (y, ym_), 1)
    y_last(2)
    sib_got(1, (2, 3))
    plan_piece(1 - zh, (yp_, (y + 2) % 4), 0)
    sib_got(2, (2, 3))
    plan_piece(1 - zh, (yp_, (y + 2) % 4), 1)

    mine = st.at[t_me]
    mass_part = jnp.sum(acc[0:8, :], axis=0, keepdims=True)
    dots_part = jnp.sum(acc[8:16, :], axis=0, keepdims=True)
    for k in range(4):
        mine[k : k + 1, :] = mass_part[:, k * 128 : (k + 1) * 128]
        mine[k + 4 : k + 5, :] = dots_part[:, k * 128 : (k + 1) * 128]
    for k in range(1, 16):
        send(f"st{k}", mine, mine, text_peers[k - 1])

    loop(4, lambda k: prep_rows(1 - zh, k))

    def right_x(k, _):
        cols = pl.ds(pl.multiple_of(k * 128, 128), 128)
        hi, lo = halves(jnp.transpose(xg[:, cols]) * SCALE)
        rows = pl.ds(pl.multiple_of(F + k * 128, 128), 128)
        rh[rows, :] = hi
        rl[rows, :] = lo
        return 0

    def right_g(k, _):
        cols = pl.ds(pl.multiple_of(F + k * 128, 128), 128)
        hi, lo = halves(jnp.transpose(xg[:, cols]))
        rows = pl.ds(pl.multiple_of(k * 128, 128), 128)
        rh[rows, :] = hi
        rl[rows, :] = lo
        return 0

    lax.fori_loop(0, 4, right_x, 0)
    lax.fori_loop(0, 4, right_g, 0)

    for k in range(1, 16):
        got(f"st{k}", st.at[(t_me + 16 - k) % 16])
    total = jnp.sum(st[...], axis=0)
    mass = jnp.concatenate([total[k : k + 1, :] for k in range(4)], axis=1)
    inv = 1.0 / mass
    dots = jnp.concatenate([total[k : k + 1, :] for k in range(4, 8)], axis=1) / mass

    def rows_of(q, d):
        zq, yd = zq_of(q), (y + d) % 4
        return zq, yd, pl.ds(pl.multiple_of((zq * 4 + yd) * 256, 256), 256)

    def weigh(q, d):
        zq, yd, rows = rows_of(q, d)
        sh = pm[zq, yd].reshape(256, F) * inv
        w_hi, w_lo = halves(sh * (gdm[zq, yd].reshape(256, F) - dots))
        wh[rows, :] = w_hi
        wl[rows, :] = w_lo
        return sh, w_hi, w_lo

    def text_block(q, d):
        zq, yd, rows = rows_of(q, d)
        if q == 1:
            sh, w_hi, w_lo = weigh(q, d)
        else:
            sh, w_hi, w_lo = pm[zq, yd].reshape(256, F) * inv, wh[rows, :], wl[rows, :]
        sh_hi, sh_lo = halves(sh)
        out = dot(
            jnp.concatenate([sh_hi, w_hi, sh_lo, w_lo, sh_hi, w_hi], axis=1),
            jnp.concatenate([rh[...], rh[...], rl[...]], axis=0),
        )
        cp[zq, yd] = out.reshape(2, TB, D)
        send(f"cs{q}{d}", cp.at[zq, yd, 1 - c], sbuf.at[q, d], sib)

    def chip_sum(q, d):
        got(f"cs{q}{d}", sbuf.at[q, d])
        return cp[zq_of(q), (y + d) % 4, c] + sbuf[q, d]

    def upper(p):
        return pl.ds(64 * p, 32)

    def lower(p):
        return pl.ds(64 * p + 32, 32)

    def far_y(q):
        ys[q, 2] = chip_sum(q, 2)
        for p in range(2):
            send(f"ra{q}{p}", ys.at[q, 2, upper(p)], ry2.at[q, p, 0], up_y)
            send(f"rb{q}{p}", ys.at[q, 2, lower(p)], ry2.at[q, p, 1], dn_y)

    def near_sums(q):
        ys[q, 1] = chip_sum(q, 1)
        ys[q, 3] = chip_sum(q, 3)

    def free_y(q, p):
        send(f"re{q}{p}", ys.at[q, 1, lower(p)], ry1.at[q, 0, lower(p)], up_y)
        send(f"rf{q}{p}", ys.at[q, 3, upper(p)], ry1.at[q, 1, upper(p)], dn_y)

    def near_y(q, p):
        got(f"ra{q}{p}", ry2.at[q, p, 0])
        ys[q, 1, upper(p)] += ry2[q, p, 0]
        send(f"rc{q}{p}", ys.at[q, 1, upper(p)], ry1.at[q, 0, upper(p)], up_y)
        got(f"rb{q}{p}", ry2.at[q, p, 1])
        ys[q, 3, lower(p)] += ry2[q, p, 1]
        send(f"rd{q}{p}", ys.at[q, 3, lower(p)], ry1.at[q, 1, lower(p)], dn_y)

    def own_y(q, p):
        got(f"re{q}{p}", ry1.at[q, 0, lower(p)])
        got(f"rf{q}{p}", ry1.at[q, 1, upper(p)])
        got(f"rc{q}{p}", ry1.at[q, 0, upper(p)])
        got(f"rd{q}{p}", ry1.at[q, 1, lower(p)])
        rows = pl.ds(64 * p, 64)
        ys[q, 0, rows] += ry1[q, 0, rows] + ry1[q, 1, rows]

    def own_z(p):
        own_y(1, p)
        rows = pl.ds(64 * p, 64)
        send(f"w{p}", ys.at[1, 0, rows], zr.at[rows], far_z)

    def speech_rows(m):
        rows = pl.ds(m * 256, 256)
        hi, lo = tth[rows, :], ttl[rows, :]
        out = dot(
            jnp.concatenate([hi, lo, hi], axis=1),
            jnp.concatenate([wh[...], wh[...], wl[...]], axis=0),
        )
        sp[pl.ds(m * 2, 2)] = out.reshape(2, 4, 32, F)

    x2 = (x + 2) % 4
    top, low = pl.ds(0, 16), pl.ds(16, 16)

    def far_x(m):
        two = pl.ds(2 * m, 2)
        send(f"ua{m}", sp.at[two, x2, top], rx2.at[0, two], up_x)
        send(f"ub{m}", sp.at[two, x2, low], rx2.at[1, two], dn_x)
        send(f"ue{m}", sp.at[two, xp_, low], rx1.at[0, two, low], up_x)
        send(f"uf{m}", sp.at[two, xm_, top], rx1.at[1, two, top], dn_x)

    def near_x(m):
        two = pl.ds(2 * m, 2)
        got(f"ua{m}", rx2.at[0, two])
        xs[0, two] = sp[two, xp_, 0:16] + rx2[0, two]
        send(f"uc{m}", xs.at[0, two], rx1.at[0, two, top], up_x)
        got(f"ub{m}", rx2.at[1, two])
        xs[1, two] = sp[two, xm_, 16:32] + rx2[1, two]
        send(f"ud{m}", xs.at[1, two], rx1.at[1, two, low], dn_x)

    def own_x(m):
        two = pl.ds(2 * m, 2)
        got(f"ue{m}", rx1.at[0, two, low])
        got(f"uf{m}", rx1.at[1, two, top])
        got(f"uc{m}", rx1.at[0, two, top])
        got(f"ud{m}", rx1.at[1, two, low])
        xo[two] = sp[two, x] + (rx1[0, two] + rx1[1, two])

    text_block(1, 2)
    text_block(1, 1)
    far_y(1)
    text_block(1, 3)
    text_block(1, 0)
    near_sums(1)
    free_y(1, 0)
    loop(4, lambda k: weigh(0, k))
    speech_rows(0)
    near_y(1, 0)
    free_y(1, 1)
    far_x(0)
    near_y(1, 1)
    ys[1, 0] = chip_sum(1, 0)
    speech_rows(1)
    far_x(1)
    text_block(0, 2)
    own_z(0)
    text_block(0, 1)
    far_y(0)
    own_z(1)
    near_x(0)
    text_block(0, 3)
    near_x(1)
    text_block(0, 0)
    near_sums(0)
    free_y(0, 0)
    free_y(0, 1)
    near_y(0, 0)
    near_y(0, 1)
    ys[0, 0] = chip_sum(0, 0)
    own_x(0)
    own_x(1)
    for r in (1, 2, 3):
        zt = (zl + r) % 4
        send(f"v{r}", xo.at[zt], rz.at[r - 1], dev(zh, y, c, zt, x))
    own_y(0, 0)
    own_y(0, 1)
    for p in range(2):
        got(f"w{p}", zr.at[pl.ds(64 * p, 64)])
    tg_ref[...] = ys[0, 0] + zr[...]
    for r in (1, 2, 3):
        got(f"v{r}", rz.at[r - 1])
    sg_ref[...] = (xo[zl] + (rz[0] + (rz[1] + rz[2]))) * SCALE
    for j in (1, 2, 3):
        for fits, one in (line_up(j), line_down(j)):

            @pl.when(fits)
            def _(one=one):
                one.wait_send()

    for one in pending:
        one.wait_send()


def finish(sg_ref, tg_ref, sg_out, tg_out):
    sg_out[...] = sg_ref[...]
    tg_out[...] = tg_ref[...]


def solution(mesh):
    def v(shape, kind=F32):
        return pltpu.VMEM(shape, kind)

    scratch = [
        v((D, 2 * F)), v((2, 4, 2, TB, D)), v((D, 2 * F), BF), v((D, 2 * F), BF),
        v((D, T), BF), v((D, T), BF), v((2 * F, D), BF), v((2 * F, D), BF),
        v((16, TB, 128)), v((2, 4, 2, TB, F)), v((2, 4, 2, TB, F)), v((T, F), BF), v((T, F), BF), v((16, F)), v((16, 8, 128)),
        v((2, 4, 2, TB, D)), v((2, 4, TB, D)), v((2, 4, TB, D)), v((2, 2, 2, 32, D)), v((2, 2, TB, D)),
        v((TB, D)), v((3, 2, 32, D)), v((3, 2, 32, D)),
        v((4, 4, 32, F)), v((2, 4, 16, F)), v((4, 32, F)), v((2, 4, 16, F)), v((2, 4, 32, F)), v((3, 32, F)),
        pltpu.SemaphoreType.DMA((len(NAMES),)),
        pltpu.SemaphoreType.DMA((len(NAMES),)),
        pltpu.SemaphoreType.DMA((3,)),
    ]
    anywhere = pl.BlockSpec(memory_space=pl.ANY)
    vmem = pl.BlockSpec(memory_space=pltpu.VMEM)
    call = pl.pallas_call(
        kernel,
        out_shape=(jax.ShapeDtypeStruct((32, F), F32), jax.ShapeDtypeStruct((TB, D), F32)),
        in_specs=[anywhere, anywhere, anywhere, vmem],
        out_specs=(vmem, vmem),
        scratch_shapes=scratch,
        compiler_params=pltpu.CompilerParams(
            collective_id=0, has_side_effects=True, vmem_limit_bytes=62 * 1024 * 1024
        ),
    )

    last = pl.pallas_call(
        finish,
        out_shape=(jax.ShapeDtypeStruct((32, F), F32), jax.ShapeDtypeStruct((TB, D), F32)),
        in_specs=[vmem, vmem],
        out_specs=(vmem, vmem),
    )

    def shards(speech_feat, text_feat, text_pot, map_grad):
        sg, tg = last(*call(speech_feat.T, map_grad.T, text_feat, text_pot.reshape(16, 128)))
        return sg.T, tg

    return jax.shard_map(
        shards,
        mesh=mesh,
        in_specs=(P("speech", "text"), P(("text", "speech"), None), P("text"), P("speech", "text")),
        out_specs=(P("speech", "text"), P(("text", "speech"), None)),
        check_vma=False,
    )
```

time: 103 us -> 86.6 us (0.84)
  the two profiles are of different devices: /device:TPU:2 before, /device:TPU:1 now
where the time goes in v1:
time: 86.6 us; the launch traced here: 86.4 us
  Pallas kernels  85.8 us (99%)
    pallas_call x1, Pallas kernels, shards(): call(speech_feat.T, map_grad.T, text_feat, text_pot.reshape(16, 128))  84.1 us

profile of v1, /device:TPU:1, one launch (start us, length us, event | category | flops | bytes accessed | tf_op | source)
XLA Modules:
  0.0 86.4 jit_solution(10682514300348072508)
XLA Ops:
  0.6 84.1 %shard_map.59 = (f32[32,512]{1,0:T(8,128)}, f32[128,512]{1,0:T(8,128)}) custom-call(f32[32,512]{1,0:T(8,128)} %bitcast.4, f32[32,512]{1,0:T(8,128)} %bitcast.5, f32[128,512]{1,0:T(8,128)} %t_ref.1, f32[16,128]{1,0:T(8,128)} %bitcast.6), custom_call_target="tpu_custom_call" | custom-call | tf_op jit(solution)/shard_map/pallas_call | solution.py:568
  84.7 1.7 %shard_map.60 = (f32[32,512]{1,0:T(8,128)}, f32[128,512]{1,0:T(8,128)}) custom-call(f32[32,512]{1,0:T(8,128)} %get-tuple-element.6.sg_ref, f32[128,512]{1,0:T(8,128)} %get-tuple-element.7.tg_ref), custom_call_target="tpu_custom_call" | custom-call | tf_op jit(solution)/shard_map/pallas_call | solution.py:568

commit v2 on v1

--- a/solution.py
+++ b/solution.py
@@ -23,8 +23,8 @@
     + [f"{k}{q}" for q in range(3) for k in ("yp", "ym", "fyp", "fym", "sb0", "sb1", "sb2", "sb3")]
     + [f"st{k}" for k in range(1, 16)]
     + [f"cs{q}{d}" for q in range(2) for d in range(4)]
-    + [f"{k}{q}{p}" for q in range(2) for p in range(2) for k in ("ra", "rb", "rc", "rd", "re", "rf")]
-    + [f"w{p}" for p in range(2)]
+    + [f"{k}{p}" for p in range(2) for k in ("ra", "rb", "rc", "rd", "re", "rf")]
+    + [f"{k}{p}" for p in range(4) for k in ("qf", "qu", "qd", "w")]
     + [f"{k}{m}" for m in range(2) for k in ("ua", "ub", "uc", "ud", "ue", "uf")]
     + ["v1", "v2", "v3"]
 )
@@ -43,7 +43,7 @@
 def kernel(
     x_ref, g_ref, t_ref, pot_ref, sg_ref, tg_ref,
     xg, tb, xh, xl, tth, ttl, rh, rl, potb, pm, gdm, wh, wl, acc, st,
-    cp, sbuf, ys, ry2, ry1, zr, ru, rd,
+    cp, sbuf, ys, ry2, ry1, qfar, zr, ru, rd,
     sp, xs, xo, rx2, rx1, rz,
     ssem, rsem, lsem,
 ):
@@ -98,16 +98,12 @@
     for one in local:
         one.start()
     barrier = pltpu.get_barrier_semaphore()
-    text_peers = []
-    for k in range(1, 16):
-        to = {"speech": s_me, "text": (t_me + k) % 16}
-        text_peers.append(to)
-        pl.semaphore_signal(barrier, inc=1, device_id=to, device_id_type=MESH)
-    for to in (sib, up_y, dn_y, far_z, up_z, dn_z):
+    text_peers = [{"speech": s_me, "text": (t_me + k) % 16} for k in range(1, 16)]
+    for to in (sib, up_y, dn_y, up_x, dn_x, up_z, dn_z):
         pl.semaphore_signal(barrier, inc=1, device_id=to, device_id_type=MESH)
     for one in local:
         one.wait()
-    pl.semaphore_wait(barrier, 21)
+    pl.semaphore_wait(barrier, 7)
 
     def line_up(j):
         block = xg_at(zl + 1 - j, x)
@@ -314,12 +310,12 @@
     plan_block(zh, 1)
     y_forward(2)
     loop(2, lambda k: plan_block(zh, k + 2))
+    y_last(1)
     sib_got(1, (0, 1))
     plan_piece(1 - zh, (y, ym_), 0)
-    y_last(1)
+    y_last(2)
     sib_got(2, (0, 1))
     plan_piece(1 - zh, (y, ym_), 1)
-    y_last(2)
     sib_got(1, (2, 3))
     plan_piece(1 - zh, (yp_, (y + 2) % 4), 0)
     sib_got(2, (2, 3))
@@ -398,39 +394,52 @@
     def lower(p):
         return pl.ds(64 * p + 32, 32)
 
-    def far_y(q):
-        ys[q, 2] = chip_sum(q, 2)
+    def far_y():
+        ys[0, 2] = chip_sum(0, 2)
         for p in range(2):
-            send(f"ra{q}{p}", ys.at[q, 2, upper(p)], ry2.at[q, p, 0], up_y)
-            send(f"rb{q}{p}", ys.at[q, 2, lower(p)], ry2.at[q, p, 1], dn_y)
-
-    def near_sums(q):
-        ys[q, 1] = chip_sum(q, 1)
-        ys[q, 3] = chip_sum(q, 3)
-
-    def free_y(q, p):
-        send(f"re{q}{p}", ys.at[q, 1, lower(p)], ry1.at[q, 0, lower(p)], up_y)
-        send(f"rf{q}{p}", ys.at[q, 3, upper(p)], ry1.at[q, 1, upper(p)], dn_y)
-
-    def near_y(q, p):
-        got(f"ra{q}{p}", ry2.at[q, p, 0])
-        ys[q, 1, upper(p)] += ry2[q, p, 0]
-        send(f"rc{q}{p}", ys.at[q, 1, upper(p)], ry1.at[q, 0, upper(p)], up_y)
-        got(f"rb{q}{p}", ry2.at[q, p, 1])
-        ys[q, 3, lower(p)] += ry2[q, p, 1]
-        send(f"rd{q}{p}", ys.at[q, 3, lower(p)], ry1.at[q, 1, lower(p)], dn_y)
-
-    def own_y(q, p):
-        got(f"re{q}{p}", ry1.at[q, 0, lower(p)])
-        got(f"rf{q}{p}", ry1.at[q, 1, upper(p)])
-        got(f"rc{q}{p}", ry1.at[q, 0, upper(p)])
-        got(f"rd{q}{p}", ry1.at[q, 1, lower(p)])
+            send(f"ra{p}", ys.at[0, 2, upper(p)], ry2.at[p, 0], up_y)
+            send(f"rb{p}", ys.at[0, 2, lower(p)], ry2.at[p, 1], dn_y)
+
+    def free_y():
+        ys[0, 1] = chip_sum(0, 1)
+        ys[0, 3] = chip_sum(0, 3)
+        for p in range(2):
+            send(f"re{p}", ys.at[0, 1, lower(p)], ry1.at[0, 0, lower(p)], up_y)
+            send(f"rf{p}", ys.at[0, 3, upper(p)], ry1.at[0, 1, upper(p)], dn_y)
+
+    def near_y(p):
+        got(f"ra{p}", ry2.at[p, 0])
+        ys[0, 1, upper(p)] += ry2[p, 0]
+        send(f"rc{p}", ys.at[0, 1, upper(p)], ry1.at[0, 0, upper(p)], up_y)
+        got(f"rb{p}", ry2.at[p, 1])
+        ys[0, 3, lower(p)] += ry2[p, 1]
+        send(f"rd{p}", ys.at[0, 3, lower(p)], ry1.at[0, 1, lower(p)], dn_y)
+
+    def own_y(p):
+        got(f"re{p}", ry1.at[0, 0, lower(p)])
+        got(f"rf{p}", ry1.at[0, 1, upper(p)])
+        got(f"rc{p}", ry1.at[0, 0, upper(p)])
+        got(f"rd{p}", ry1.at[0, 1, lower(p)])
         rows = pl.ds(64 * p, 64)
-        ys[q, 0, rows] += ry1[q, 0, rows] + ry1[q, 1, rows]
+        ys[0, 0, rows] += ry1[0, 0, rows] + ry1[0, 1, rows]
+
+    def piece(p):
+        return pl.ds(32 * p, 32)
+
+    def straight(name, d, p):
+        to, dst = {
+            "qf": (dev(zh, (y + 2) % 4, c, zl, x), qfar),
+            "qu": (up_y, ry1.at[1, 0]),
+            "qd": (dn_y, ry1.at[1, 1]),
+        }[name]
+        send(f"{name}{p}", ys.at[1, d, piece(p)], dst.at[piece(p)], to)
 
     def own_z(p):
-        own_y(1, p)
-        rows = pl.ds(64 * p, 64)
+        rows = piece(p)
+        got(f"qf{p}", qfar.at[rows])
+        got(f"qu{p}", ry1.at[1, 0, rows])
+        got(f"qd{p}", ry1.at[1, 1, rows])
+        ys[1, 0, rows] += qfar[rows] + (ry1[1, 0, rows] + ry1[1, 1, rows])
         send(f"w{p}", ys.at[1, 0, rows], zr.at[rows], far_z)
 
     def speech_rows(m):
@@ -471,44 +480,48 @@
 
     text_block(1, 2)
     text_block(1, 1)
-    far_y(1)
+    ys[1, 2] = chip_sum(1, 2)
+    straight("qf", 2, 0)
     text_block(1, 3)
+    ys[1, 1] = chip_sum(1, 1)
+    straight("qu", 1, 0)
     text_block(1, 0)
-    near_sums(1)
-    free_y(1, 0)
+    ys[1, 3] = chip_sum(1, 3)
+    straight("qd", 3, 0)
+    for p in range(1, 4):
+        straight("qf", 2, p)
+        straight("qu", 1, p)
+        straight("qd", 3, p)
     loop(4, lambda k: weigh(0, k))
+    ys[1, 0] = chip_sum(1, 0)
     speech_rows(0)
-    near_y(1, 0)
-    free_y(1, 1)
     far_x(0)
-    near_y(1, 1)
-    ys[1, 0] = chip_sum(1, 0)
+    text_block(0, 2)
+    own_z(0)
     speech_rows(1)
     far_x(1)
-    text_block(0, 2)
-    own_z(0)
+    own_z(1)
     text_block(0, 1)
-    far_y(0)
-    own_z(1)
+    far_y()
     near_x(0)
     text_block(0, 3)
+    own_z(2)
     near_x(1)
     text_block(0, 0)
-    near_sums(0)
-    free_y(0, 0)
-    free_y(0, 1)
-    near_y(0, 0)
-    near_y(0, 1)
-    ys[0, 0] = chip_sum(0, 0)
+    free_y()
+    own_z(3)
     own_x(0)
+    near_y(0)
+    near_y(1)
     own_x(1)
     for r in (1, 2, 3):
         zt = (zl + r) % 4
         send(f"v{r}", xo.at[zt], rz.at[r - 1], dev(zh, y, c, zt, x))
-    own_y(0, 0)
-    own_y(0, 1)
-    for p in range(2):
-        got(f"w{p}", zr.at[pl.ds(64 * p, 64)])
+    ys[0, 0] = chip_sum(0, 0)
+    own_y(0)
+    own_y(1)
+    for p in range(4):
+        got(f"w{p}", zr.at[piece(p)])
     tg_ref[...] = ys[0, 0] + zr[...]
     for r in (1, 2, 3):
         got(f"v{r}", rz.at[r - 1])
@@ -537,7 +550,7 @@
         v((D, 2 * F)), v((2, 4, 2, TB, D)), v((D, 2 * F), BF), v((D, 2 * F), BF),
         v((D, T), BF), v((D, T), BF), v((2 * F, D), BF), v((2 * F, D), BF),
         v((16, TB, 128)), v((2, 4, 2, TB, F)), v((2, 4, 2, TB, F)), v((T, F), BF), v((T, F), BF), v((16, F)), v((16, 8, 128)),
-        v((2, 4, 2, TB, D)), v((2, 4, TB, D)), v((2, 4, TB, D)), v((2, 2, 2, 32, D)), v((2, 2, TB, D)),
+        v((2, 4, 2, TB, D)), v((2, 4, TB, D)), v((2, 4, TB, D)), v((2, 2, 32, D)), v((2, 2, TB, D)), v((TB, D)),
         v((TB, D)), v((3, 2, 32, D)), v((3, 2, 32, D)),
         v((4, 4, 32, F)), v((2, 4, 16, F)), v((4, 32, F)), v((2, 4, 16, F)), v((2, 4, 32, F)), v((3, 32, F)),
         pltpu.SemaphoreType.DMA((len(NAMES),)),

time: 86.6 us -> 84.2 us (0.972)
  Pallas kernels: 85.8 us -> 83.4 us
    pallas_call x1, Pallas kernels: 84.1 us -> 81.6 us  [shards(): call(speech_feat.T, map_grad.T, text_feat, text_pot.reshape(16, 128))]
where the time goes in v2:
time: 84.2 us; the launch traced here: 84 us
  Pallas kernels  83.4 us (99%)
    pallas_call x1, Pallas kernels, shards(): call(speech_feat.T, map_grad.T, text_feat, text_pot.reshape(16, 128))  81.6 us
    pallas_call x1, Pallas kernels, shards(): last(*call(speech_feat.T, map_grad.T, text_feat, text_pot.reshape(16, 128)))  1.72 us

profile of v2, /device:TPU:1, one launch (start us, length us, event | category | flops | bytes accessed | tf_op | source)
XLA Modules:
  0.0 84.0 jit_solution(640256891039237079)
XLA Ops:
  0.6 81.6 %shard_map.59 = (f32[32,512]{1,0:T(8,128)}, f32[128,512]{1,0:T(8,128)}) custom-call(f32[32,512]{1,0:T(8,128)} %bitcast.4, f32[32,512]{1,0:T(8,128)} %bitcast.5, f32[128,512]{1,0:T(8,128)} %t_ref.1, f32[16,128]{1,0:T(8,128)} %bitcast.6), custom_call_target="tpu_custom_call" | custom-call | tf_op jit(solution)/shard_map/pallas_call | solution.py:581
  82.3 1.7 %shard_map.60 = (f32[32,512]{1,0:T(8,128)}, f32[128,512]{1,0:T(8,128)}) custom-call(f32[32,512]{1,0:T(8,128)} %get-tuple-element.6.sg_ref, f32[128,512]{1,0:T(8,128)} %get-tuple-element.7.tg_ref), custom_call_target="tpu_custom_call" | custom-call | tf_op jit(solution)/shard_map/pallas_call | solution.py:581

commit v3 on v2

v3 whole, which is shorter than its diff:
```python
import math

import jax
import jax.numpy as jnp
from jax import lax
from jax.experimental import pallas as pl
from jax.experimental.pallas import tpu as pltpu
from jax.sharding import PartitionSpec as P

D = 512
F = 512
T = 2048
TB = 128
SCALE = 1.0 / math.sqrt(D)
BF = jnp.bfloat16
F32 = jnp.float32
MESH = pl.DeviceIdType.MESH

GROUPS = (
    ["xf", "st", "v", "w", "sb0"]
    + [f"x{r}" for r in range(4)]
    + [f"z{k}{j}" for k in "ud" for j in (1, 2, 3)]
    + [f"t{h}{p}" for h in (1, 2, 3, 4) for p in range(4)]
    + [f"{k}{g}" for g in range(5) for k in ("y", "yf", "sbn", "sbf") if g or k[0] == "y"]
    + [f"{k}{p}" for p in range(4) for k in ("cs", "ct")]
    + [f"{k}{p}" for p in range(2) for k in ("ra", "rb", "ua", "ub")]
    + [f"q{n}" for n in range(5)]
)
KINDS = ["x", "t", "y", "yy", "st", "c", "r", "q", "u", "v"] + [f"z{k}{j}" for k in "ud" for j in (1, 2, 3)]
GROUP = {name: k for k, name in enumerate(GROUPS)}
KIND = {name: k for k, name in enumerate(KINDS)}
PARTS = ((0, 16), (16, 16), (32, 32), (64, 32), (96, 32))


def halves(v):
    hi = v.astype(BF)
    return hi, (v - hi.astype(F32)).astype(BF)


def dot(a, b):
    return lax.dot_general(a, b, (((1,), (0,)), ((), ())), preferred_element_type=F32)


def kernel(
    x_ref, g_ref, t_ref, pot_ref, sg_ref, tg_ref,
    xg, tb, xh, xl, tth, ttl, rh, rl, potb, pm, gdm, wh, wl, acc, st,
    cp, sbuf, ys, ry2, ry1, qfar, zr, ru, rd,
    sp, xs, xo, rx2, rx1, rz,
    ssem, rsem, lsem,
):
    s_me = lax.axis_index("speech")
    t_me = lax.axis_index("text")
    zh, y, c = s_me // 8, (s_me // 2) % 4, s_me % 2
    zl, x = t_me // 4, t_me % 4
    z = zh * 4 + zl

    def dev(zh_, y_, c_, zl_, x_):
        return {"speech": (zh_ * 4 + y_) * 2 + c_, "text": zl_ * 4 + x_}

    def at_z(zz):
        return dev(zz // 4, y, c, zz % 4, x)

    yp_, ym_ = (y + 1) % 4, (y + 3) % 4
    xp_, xm_ = (x + 1) % 4, (x + 3) % 4
    sib = dev(zh, y, 1 - c, zl, x)
    up_y, dn_y = dev(zh, yp_, c, zl, x), dev(zh, ym_, c, zl, x)
    up_x, dn_x = dev(zh, y, c, zl, xp_), dev(zh, y, c, zl, xm_)
    far_z = at_z((z + 4) % 8)
    up_z, dn_z = at_z((z + 1) % 8), at_z((z + 7) % 8)

    sent = dict.fromkeys(KINDS, 0)

    def copy(kind, group, src, dst, to):
        return pltpu.make_async_remote_copy(
            src_ref=src,
            dst_ref=dst,
            send_sem=ssem.at[KIND[kind]],
            recv_sem=rsem.at[GROUP[group]],
            device_id=to,
            device_id_type=MESH,
        )

    def send(kind, group, src, dst, to, track=True):
        copy(kind, group, src, dst, to).start()
        if track:
            sent[kind] += math.prod(src.shape) * 4

    def bulk(size):
        return st.at[pl.ds(0, 15)] if size == 61440 else xg.at[pl.ds(0, size // 4096), :]

    def got(group, ref):
        copy("x", group, ref, ref, sib).wait_recv()

    def got_kb(group, kb):
        got(group, bulk(kb * 1024))

    def xg_at(zl_, x_, lo=0, n=32):
        return xg.at[pl.ds(pl.multiple_of((zl_ * 4 + x_) * 32 + lo, 16), n), :]

    def tb_at(zh_, y_, c_, lo=0, n=TB):
        return tb.at[zh_, y_, c_, pl.ds(lo, n), :]

    own_rows = pl.ds(pl.multiple_of(t_me * 32, 32), 32)
    local = [
        pltpu.make_async_copy(x_ref, xg.at[own_rows, pl.ds(0, F)], lsem.at[0]),
        pltpu.make_async_copy(g_ref, xg.at[own_rows, pl.ds(F, F)], lsem.at[1]),
        pltpu.make_async_copy(t_ref, tb_at(zh, y, c), lsem.at[2]),
    ]
    for one in local:
        one.start()
    barrier = pltpu.get_barrier_semaphore()
    text_peers = [{"speech": s_me, "text": (t_me + k) % 16} for k in range(1, 16)]
    for to in (sib, up_y, dn_y, up_x, dn_x, up_z, dn_z):
        pl.semaphore_signal(barrier, inc=1, device_id=to, device_id_type=MESH)
    for one in local:
        one.wait()
    pl.semaphore_wait(barrier, 7)

    def line_up(j):
        block = xg_at(zl + 1 - j, x)
        return (zl <= 2) & (zl >= j - 1), copy(f"zu{j}", f"zu{j}", block, block, dev(zh, y, c, zl + 1, x))

    def line_down(j):
        block = xg_at(zl + j - 1, x)
        return (zl >= 1) & (zl <= 4 - j), copy(f"zd{j}", f"zd{j}", block, block, dev(zh, y, c, zl - 1, x))

    def line_send(j):
        for fits, one in (line_up(j), line_down(j)):

            @pl.when(fits)
            def _(one=one):
                one.start()

    def line_got(j):
        @pl.when(zl >= j)
        def _():
            got(f"zu{j}", xg_at(zl - j, x))

        @pl.when(zl <= 3 - j)
        def _():
            got(f"zd{j}", xg_at(zl + j, x))

    def line_step(j):
        line_got(j)
        if j < 3:
            line_send(j + 1)
        by_step(j, x_send)

    def by_step(j, do):
        if j == 2:
            do(2)
            return
        for r, here in ((1, zl >= 1), (3, zl <= 2)) if j == 1 else ((3, zl == 3), (1, zl == 0)):

            @pl.when(here)
            def _(r=r):
                do(r, False)

    def x_send(r, track=True):
        zs = (zl + 4 - r) % 4
        send("x", f"x{r}", xg_at(zs, x), xg_at(zs, x), up_x, track)
        send("x", f"x{r}", xg_at(zs, x), xg_at(zs, x), dn_x, track)

    def x_forward(r, track=True):
        zs = (zl + 4 - r) % 4
        got_kb(f"x{r}", 256)
        send("x", "xf", xg_at(zs, xm_, 0, 16), xg_at(zs, xm_, 0, 16), up_x, track)
        send("x", "xf", xg_at(zs, xp_, 16, 16), xg_at(zs, xp_, 16, 16), dn_x, track)

    def zq_of(q):
        return zh if q == 0 else 1 - zh

    def parcel(g):
        return (zh, 0, TB) if g == 0 else (1 - zh, (g - 1) * 32, 32)

    def yk(g):
        return "yy" if g else "y"

    def sb(g, k):
        return "sb0" if g == 0 else f"sbf{g}" if k > 1 else f"sbn{g}"

    def y_send(g):
        zq, lo, n = parcel(g)
        send(yk(g), f"y{g}", tb_at(zq, y, c, lo, n), tb_at(zq, y, c, lo, n), up_y)
        send(yk(g), f"y{g}", tb_at(zq, y, c, lo, n), tb_at(zq, y, c, lo, n), dn_y)
        send(yk(g), sb(g, 0), tb_at(zq, y, c, lo, n), tb_at(zq, y, c, lo, n), sib)

    def y_forward(g):
        zq, lo, n = parcel(g)
        h = n // 2
        got_kb(f"y{g}", 4 * n)
        send(yk(g), f"yf{g}", tb_at(zq, ym_, c, lo, h), tb_at(zq, ym_, c, lo, h), up_y)
        send(yk(g), f"yf{g}", tb_at(zq, yp_, c, lo + h, h), tb_at(zq, yp_, c, lo + h, h), dn_y)
        send(yk(g), sb(g, 1), tb_at(zq, ym_, c, lo, n), tb_at(zq, ym_, c, lo, n), sib)
        send(yk(g), sb(g, 2), tb_at(zq, yp_, c, lo, n), tb_at(zq, yp_, c, lo, n), sib)

    def y_last(g):
        zq, lo, n = parcel(g)
        h, y2 = n // 2, (y + 2) % 4
        got(f"yf{g}", tb_at(zq, y2, c, lo, n))
        send(yk(g), sb(g, 3), tb_at(zq, y2, c, lo, n), tb_at(zq, y2, c, lo, n), sib)

    def sib_got(g, far=False):
        if g == 0:
            got_kb("sb0", 1024)
        else:
            got_kb(sb(g, 2 if far else 0), 128)

    def t_hop(h):
        for p in range(4):
            u, d = pl.ds(32 * p, 16), pl.ds(32 * p + 16, 16)
            if h == 1:
                src_u, src_d = tb.at[zh, y, c, u], tb.at[zh, y, c, d]
            else:
                src_u, src_d = ru.at[h - 2, p], rd.at[h - 2, p]
                got_kb(f"t{h - 1}{p}", 64)
            if h == 4:
                dst_u, dst_d = tb.at[((z + 5) % 8) // 4, y, c, u], tb.at[((z + 3) % 8) // 4, y, c, d]
            else:
                dst_u, dst_d = ru.at[h - 1, p], rd.at[h - 1, p]
            send("t", f"t{h}{p}", src_u, dst_u, up_z)
            send("t", f"t{h}{p}", src_d, dst_d, dn_z)

    def z_arrived(p):
        got(f"t4{p}", tb_at(1 - zh, y, c, 32 * p, 32))
        y_send(p + 1)

    line_send(1)
    x_send(0)
    t_hop(1)
    y_send(0)

    def pot_step(k, _):
        row = jnp.broadcast_to(pot_ref[pl.ds(k, 1), :], (128, 128))
        potb[k] = jnp.transpose(row)
        return 0

    lax.fori_loop(0, 16, pot_step, 0)

    def prep_rows(zq, yy):
        hi, lo = halves(jnp.transpose(tb[zq, yy].reshape(256, D)))
        cols = pl.ds(pl.multiple_of((zq * 4 + yy) * 256, 256), 256)
        tth[:, cols] = hi
        ttl[:, cols] = lo

    def split_x(k, _):
        rows = pl.ds(pl.multiple_of(k * 64, 64), 64)
        hi, lo = halves(xg[rows, :])
        xh[rows, :] = hi
        xl[rows, :] = lo
        return 0

    def plan_part(rows_t, pot, put):
        hi, lo = halves(rows_t)
        prod = dot(
            jnp.concatenate([hi, lo, hi], axis=1),
            jnp.concatenate([xh[...], xh[...], xl[...]], axis=0),
        )
        p = jnp.exp(prod[:, :F] * SCALE + jnp.concatenate([pot] * 4, axis=1))
        gd = prod[:, F:]
        put(p, gd)
        acc[0:8, :] += jnp.sum(p.reshape(32, 8, F), axis=0)
        acc[8:16, :] += jnp.sum((p * gd).reshape(32, 8, F), axis=0)

    def plan_block(zq, yy):
        def put(p, gd):
            pm[zq, yy] = p.reshape(2, TB, F)
            gdm[zq, yy] = gd.reshape(2, TB, F)

        pot = potb[pl.ds((zq * 4 + yy) * 2, 2)].reshape(256, 128)
        plan_part(tb[zq, yy].reshape(256, D), pot, put)

    def plan_piece(zq, two_y, p):
        rows = pl.ds(64 * p, 64)

        def put(p_, gd):
            for k, yy in enumerate(two_y):
                part = slice(128 * k, 128 * k + 128)
                pm[zq, yy, :, rows, :] = p_[part].reshape(2, 64, F)
                gdm[zq, yy, :, rows, :] = gd[part].reshape(2, 64, F)

        pot = jnp.concatenate([potb[pl.ds((zq * 4 + yy) * 2, 2), rows, :].reshape(128, 128) for yy in two_y], axis=0)
        tok = jnp.concatenate([tb[zq, yy, :, rows, :].reshape(128, D) for yy in two_y], axis=0)
        plan_part(tok, pot, put)

    def loop(n, step):
        lax.fori_loop(0, n, lambda k, _: (step(k), 0)[1], 0)

    acc[...] = jnp.zeros_like(acc)
    line_step(1)
    x_forward(0)
    t_hop(2)
    y_forward(0)
    line_step(2)
    by_step(1, x_forward)
    t_hop(3)
    y_last(0)
    line_step(3)
    by_step(2, x_forward)
    sib_got(0)
    t_hop(4)
    by_step(3, x_forward)
    loop(4, lambda k: prep_rows(zh, k))
    z_arrived(0)
    z_arrived(1)
    z_arrived(2)
    z_arrived(3)
    got_kb("xf", 512)
    lax.fori_loop(0, 8, split_x, 0)
    plan_block(zh, 0)
    y_forward(1)
    plan_block(zh, 1)
    y_forward(2)
    plan_block(zh, 2)
    y_forward(3)
    plan_block(zh, 3)
    y_forward(4)
    sib_got(1)
    sib_got(2)
    plan_piece(1 - zh, (y, ym_), 0)
    y_last(1)
    y_last(2)
    sib_got(3)
    sib_got(4)
    plan_piece(1 - zh, (y, ym_), 1)
    y_last(3)
    y_last(4)
    sib_got(1, True)
    sib_got(2, True)
    plan_piece(1 - zh, (yp_, (y + 2) % 4), 0)
    sib_got(3, True)
    sib_got(4, True)
    plan_piece(1 - zh, (yp_, (y + 2) % 4), 1)

    mine = st.at[t_me]
    mass_part = jnp.sum(acc[0:8, :], axis=0, keepdims=True)
    dots_part = jnp.sum(acc[8:16, :], axis=0, keepdims=True)
    for k in range(4):
        mine[k : k + 1, :] = mass_part[:, k * 128 : (k + 1) * 128]
        mine[k + 4 : k + 5, :] = dots_part[:, k * 128 : (k + 1) * 128]
    for k in range(1, 16):
        send("st", "st", mine, mine, text_peers[k - 1])

    loop(4, lambda k: prep_rows(1 - zh, k))

    def right_x(k, _):
        cols = pl.ds(pl.multiple_of(k * 128, 128), 128)
        hi, lo = halves(jnp.transpose(xg[:, cols]) * SCALE)
        rows = pl.ds(pl.multiple_of(F + k * 128, 128), 128)
        rh[rows, :] = hi
        rl[rows, :] = lo
        return 0

    def right_g(k, _):
        cols = pl.ds(pl.multiple_of(F + k * 128, 128), 128)
        hi, lo = halves(jnp.transpose(xg[:, cols]))
        rows = pl.ds(pl.multiple_of(k * 128, 128), 128)
        rh[rows, :] = hi
        rl[rows, :] = lo
        return 0

    lax.fori_loop(0, 4, right_x, 0)
    lax.fori_loop(0, 4, right_g, 0)

    got_kb("st", 60)
    total = jnp.sum(st[...], axis=0)
    mass = jnp.concatenate([total[k : k + 1, :] for k in range(4)], axis=1)
    inv = 1.0 / mass
    dots = jnp.concatenate([total[k : k + 1, :] for k in range(4, 8)], axis=1) / mass

    def weights(p, gd):
        sh = p * inv
        return halves(sh), halves(sh * (gd - dots))

    def right_product(sh, w):
        return dot(
            jnp.concatenate([sh[0], w[0], sh[1], w[1], sh[0], w[0]], axis=1),
            jnp.concatenate([rh[...], rh[...], rl[...]], axis=0),
        )

    def weigh(yy):
        _, w = weights(pm[zh, yy].reshape(256, F), gdm[zh, yy].reshape(256, F))
        wh[zh, yy] = w[0].reshape(2, TB, F)
        wl[zh, yy] = w[1].reshape(2, TB, F)

    def text_block(d):
        yd = (y + d) % 4
        sh = halves(pm[zh, yd].reshape(256, F) * inv)
        out = right_product(sh, (wh[zh, yd].reshape(256, F), wl[zh, yd].reshape(256, F)))
        cp[zh, yd] = out.reshape(2, TB, D)
        send("c", f"cs{d}", cp.at[zh, yd, 1 - c], sbuf.at[0, d], sib)

    def chip_sum(d):
        got(f"cs{d}", sbuf.at[0, d])
        return cp[zh, (y + d) % 4, c] + sbuf[0, d]

    def piece(p):
        return pl.ds(32 * p, 32)

    def text_piece(p):
        zq, rows = 1 - zh, piece(p)
        sh, w = weights(pm[zq, :, :, rows, :].reshape(256, F), gdm[zq, :, :, rows, :].reshape(256, F))
        wh[zq, :, :, rows, :] = w[0].reshape(4, 2, 32, F)
        wl[zq, :, :, rows, :] = w[1].reshape(4, 2, 32, F)
        cp[zq, :, :, rows, :] = right_product(sh, w).reshape(4, 2, 32, D)
        send("c", f"ct{p}", cp.at[zq, :, 1 - c, rows], sbuf.at[1, :, rows], sib)

    def straight(p):
        rows = piece(p)
        got(f"ct{p}", sbuf.at[1, :, rows])
        ys[1, :, rows] = cp[1 - zh, :, c, rows] + sbuf[1, :, rows]
        y2 = (y + 2) % 4
        for n in (0, 1) if p == 0 else (p + 1,):
            rows = pl.ds(*PARTS[n])
            send("q", f"q{n}", ys.at[1, y2, rows], qfar.at[rows], dev(zh, y2, c, zl, x))
            send("q", f"q{n}", ys.at[1, yp_, rows], ry1.at[1, 0, rows], up_y)
            send("q", f"q{n}", ys.at[1, ym_, rows], ry1.at[1, 1, rows], dn_y)

    def own_z(n):
        rows = pl.ds(*PARTS[n])
        got_kb(f"q{n}", 6 * PARTS[n][1])
        ys[1, y, rows] += qfar[rows] + (ry1[1, 0, rows] + ry1[1, 1, rows])
        send("q", "w", ys.at[1, y, rows], zr.at[rows], far_z)

    def upper(p):
        return pl.ds(64 * p, 32)

    def lower(p):
        return pl.ds(64 * p + 32, 32)

    def far_y():
        ys[0, 2] = chip_sum(2)
        for p in range(2):
            send("r", f"ra{p}", ys.at[0, 2, upper(p)], ry2.at[p, 0], up_y)
            send("r", f"ra{p}", ys.at[0, 2, lower(p)], ry2.at[p, 1], dn_y)

    def free_y():
        ys[0, 1] = chip_sum(1)
        ys[0, 3] = chip_sum(3)
        for p in range(2):
            send("r", f"rb{p}", ys.at[0, 1, lower(p)], ry1.at[0, 0, lower(p)], up_y)
            send("r", f"rb{p}", ys.at[0, 3, upper(p)], ry1.at[0, 1, upper(p)], dn_y)

    def near_y(p):
        got_kb(f"ra{p}", 128)
        ys[0, 1, upper(p)] += ry2[p, 0]
        send("r", f"rb{p}", ys.at[0, 1, upper(p)], ry1.at[0, 0, upper(p)], up_y)
        ys[0, 3, lower(p)] += ry2[p, 1]
        send("r", f"rb{p}", ys.at[0, 3, lower(p)], ry1.at[0, 1, lower(p)], dn_y)

    def own_y(p):
        got_kb(f"rb{p}", 256)
        rows = pl.ds(64 * p, 64)
        ys[0, 0, rows] += ry1[0, 0, rows] + ry1[0, 1, rows]

    def speech_rows(m):
        rows = pl.ds(m * 256, 256)
        hi, lo = tth[rows, :], ttl[rows, :]
        out = dot(
            jnp.concatenate([hi, lo, hi], axis=1),
            jnp.concatenate([wh[...].reshape(T, F), wh[...].reshape(T, F), wl[...].reshape(T, F)], axis=0),
        )
        sp[pl.ds(m * 2, 2)] = out.reshape(2, 4, 32, F)

    x2 = (x + 2) % 4
    top, low = pl.ds(0, 16), pl.ds(16, 16)

    def far_x(m):
        two = pl.ds(2 * m, 2)
        send("u", f"ua{m}", sp.at[two, x2, top], rx2.at[0, two], up_x)
        send("u", f"ua{m}", sp.at[two, x2, low], rx2.at[1, two], dn_x)
        send("u", f"ub{m}", sp.at[two, xp_, low], rx1.at[0, two, low], up_x)
        send("u", f"ub{m}", sp.at[two, xm_, top], rx1.at[1, two, top], dn_x)

    def near_x(m):
        two = pl.ds(2 * m, 2)
        got_kb(f"ua{m}", 128)
        xs[0, two] = sp[two, xp_, 0:16] + rx2[0, two]
        send("u", f"ub{m}", xs.at[0, two], rx1.at[0, two, top], up_x)
        xs[1, two] = sp[two, xm_, 16:32] + rx2[1, two]
        send("u", f"ub{m}", xs.at[1, two], rx1.at[1, two, low], dn_x)

    def own_x(m):
        two = pl.ds(2 * m, 2)
        got_kb(f"ub{m}", 256)
        xo[two] = sp[two, x] + (rx1[0, two] + rx1[1, two])

    text_piece(0)
    text_piece(1)
    straight(0)
    text_piece(2)
    straight(1)
    text_piece(3)
    straight(2)
    loop(4, weigh)
    straight(3)
    own_z(0)
    speech_rows(0)
    far_x(0)
    own_z(1)
    speech_rows(1)
    far_x(1)
    text_block(2)
    own_z(2)
    text_block(1)
    far_y()
    near_x(0)
    text_block(3)
    own_z(3)
    near_x(1)
    text_block(0)
    free_y()
    own_z(4)
    own_x(0)
    own_x(1)
    for r in (1, 2, 3):
        zt = (zl + r) % 4
        send("v", "v", xo.at[zt], rz.at[r - 1], dev(zh, y, c, zt, x))
    ys[0, 0] = chip_sum(0)
    near_y(0)
    near_y(1)
    own_y(0)
    own_y(1)
    got("w", zr)
    tg_ref[...] = ys[0, 0] + zr[...]
    got("v", rz)
    sg_ref[...] = (xo[zl] + (rz[0] + (rz[1] + rz[2]))) * SCALE
    for j in (1, 2, 3):
        for fits, one in (line_up(j), line_down(j)):

            @pl.when(fits)
            def _(one=one):
                one.wait_send()

    for r in (1, 3):
        sent["x"] += 2 * 32 * 4096 + 2 * 16 * 4096
    for kind, size in sent.items():
        if size:
            copy(kind, "x0", bulk(size), bulk(size), sib).wait_send()


def finish(sg_ref, tg_ref, sg_out, tg_out):
    sg_out[...] = sg_ref[...]
    tg_out[...] = tg_ref[...]


def solution(mesh):
    def v(shape, kind=F32):
        return pltpu.VMEM(shape, kind)

    scratch = [
        v((D, 2 * F)), v((2, 4, 2, TB, D)), v((D, 2 * F), BF), v((D, 2 * F), BF),
        v((D, T), BF), v((D, T), BF), v((2 * F, D), BF), v((2 * F, D), BF),
        v((16, TB, 128)), v((2, 4, 2, TB, F)), v((2, 4, 2, TB, F)), v((2, 4, 2, TB, F), BF), v((2, 4, 2, TB, F), BF), v((16, F)), v((16, 8, 128)),
        v((2, 4, 2, TB, D)), v((2, 4, TB, D)), v((2, 4, TB, D)), v((2, 2, 32, D)), v((2, 2, TB, D)), v((TB, D)),
        v((TB, D)), v((3, 4, 16, D)), v((3, 4, 16, D)),
        v((4, 4, 32, F)), v((2, 4, 16, F)), v((4, 32, F)), v((2, 4, 16, F)), v((2, 4, 32, F)), v((3, 32, F)),
        pltpu.SemaphoreType.DMA((len(KINDS),)),
        pltpu.SemaphoreType.DMA((len(GROUPS),)),
        pltpu.SemaphoreType.DMA((3,)),
    ]
    anywhere = pl.BlockSpec(memory_space=pl.ANY)
    vmem = pl.BlockSpec(memory_space=pltpu.VMEM)
    call = pl.pallas_call(
        kernel,
        out_shape=(jax.ShapeDtypeStruct((32, F), F32), jax.ShapeDtypeStruct((TB, D), F32)),
        in_specs=[anywhere, anywhere, anywhere, vmem],
        out_specs=(vmem, vmem),
        scratch_shapes=scratch,
        compiler_params=pltpu.CompilerParams(
            collective_id=0, has_side_effects=True, vmem_limit_bytes=62 * 1024 * 1024
        ),
    )

    last = pl.pallas_call(
        finish,
        out_shape=(jax.ShapeDtypeStruct((32, F), F32), jax.ShapeDtypeStruct((TB, D), F32)),
        in_specs=[vmem, vmem],
        out_specs=(vmem, vmem),
    )

    def shards(speech_feat, text_feat, text_pot, map_grad):
        sg, tg = last(*call(speech_feat.T, map_grad.T, text_feat, text_pot.reshape(16, 128)))
        return sg.T, tg

    return jax.shard_map(
        shards,
        mesh=mesh,
        in_specs=(P("speech", "text"), P(("text", "speech"), None), P("text"), P("speech", "text")),
        out_specs=(P("speech", "text"), P(("text", "speech"), None)),
        check_vma=False,
    )
```

time: 84.2 us -> 81.2 us (0.964)
  Pallas kernels: 83.4 us -> 80.4 us
    pallas_call x1, Pallas kernels: 81.6 us -> 78.7 us  [shards(): call(speech_feat.T, map_grad.T, text_feat, text_pot.reshape(16, 128))]
where the time goes in v3:
time: 81.2 us; the launch traced here: 81 us
  Pallas kernels  80.4 us (99%)
    pallas_call x1, Pallas kernels, shards(): call(speech_feat.T, map_grad.T, text_feat, text_pot.reshape(16, 128))  78.7 us
    pallas_call x1, Pallas kernels, shards(): last(*call(speech_feat.T, map_grad.T, text_feat, text_pot.reshape(16, 128)))  1.72 us

profile of v3, /device:TPU:1, one launch (start us, length us, event | category | flops | bytes accessed | tf_op | source)
XLA Modules:
  0.0 81.0 jit_solution(5564725135095042896)
XLA Ops:
  0.6 78.7 %shard_map.59 = (f32[32,512]{1,0:T(8,128)}, f32[128,512]{1,0:T(8,128)}) custom-call(f32[32,512]{1,0:T(8,128)} %bitcast.4, f32[32,512]{1,0:T(8,128)} %bitcast.5, f32[128,512]{1,0:T(8,128)} %t_ref.1, f32[16,128]{1,0:T(8,128)} %bitcast.6), custom_call_target="tpu_custom_call" | custom-call | tf_op jit(solution)/shard_map/pallas_call | solution.py:583
  79.3 1.7 %shard_map.60 = (f32[32,512]{1,0:T(8,128)}, f32[128,512]{1,0:T(8,128)}) custom-call(f32[32,512]{1,0:T(8,128)} %get-tuple-element.6.sg_ref, f32[128,512]{1,0:T(8,128)} %get-tuple-element.7.tg_ref), custom_call_target="tpu_custom_call" | custom-call | tf_op jit(solution)/shard_map/pallas_call | solution.py:583

commit v4 on v3

--- a/solution.py
+++ b/solution.py
@@ -513,9 +513,8 @@
     own_z(4)
     own_x(0)
     own_x(1)
-    for r in (1, 2, 3):
-        zt = (zl + r) % 4
-        send("v", "v", xo.at[zt], rz.at[r - 1], dev(zh, y, c, zt, x))
+    for k, zt in enumerate((3 - zl, (zl + 2) % 4, zl + 1 - 2 * (zl % 2))):
+        send("v", "v", xo.at[zt], rz.at[k], dev(zh, y, c, zt, x))
     ys[0, 0] = chip_sum(0)
     near_y(0)
     near_y(1)

time: 81.2 us -> 82.6 us (1.017)
  Pallas kernels: 80.4 us -> 81.8 us
    pallas_call x1, Pallas kernels: 78.7 us -> 80.1 us  [shards(): call(speech_feat.T, map_grad.T, text_feat, text_pot.reshape(16, 128))]
where the time goes in v4:
time: 82.6 us; the launch traced here: 82.4 us
  Pallas kernels  81.8 us (99%)
    pallas_call x1, Pallas kernels, shards(): call(speech_feat.T, map_grad.T, text_feat, text_pot.reshape(16, 128))  80.1 us
    pallas_call x1, Pallas kernels, shards(): last(*call(speech_feat.T, map_grad.T, text_feat, text_pot.reshape(16, 128)))  1.72 us

profile of v4, /device:TPU:1, one launch (start us, length us, event | category | flops | bytes accessed | tf_op | source)
XLA Modules:
  0.0 82.4 jit_solution(5345295412521581079)
XLA Ops:
  0.6 80.1 %shard_map.59 = (f32[32,512]{1,0:T(8,128)}, f32[128,512]{1,0:T(8,128)}) custom-call(f32[32,512]{1,0:T(8,128)} %bitcast.4, f32[32,512]{1,0:T(8,128)} %bitcast.5, f32[128,512]{1,0:T(8,128)} %t_ref.1, f32[16,128]{1,0:T(8,128)} %bitcast.6), custom_call_target="tpu_custom_call" | custom-call | tf_op jit(solution)/shard_map/pallas_call | solution.py:582
  80.7 1.7 %shard_map.60 = (f32[32,512]{1,0:T(8,128)}, f32[128,512]{1,0:T(8,128)}) custom-call(f32[32,512]{1,0:T(8,128)} %get-tuple-element.6.sg_ref, f32[128,512]{1,0:T(8,128)} %get-tuple-element.7.tg_ref), custom_call_target="tpu_custom_call" | custom-call | tf_op jit(solution)/shard_map/pallas_call | solution.py:582
